TPU v7x, 128 devices: a whole 4x4x4 slice. The times are simulated.
128 devices in a mesh: grp: 2 (over core), voc: 64 (over z, y, x).
Axes of the slice: x: 4, y: 4, z: 4, core: 2. Of those that a mesh axis runs over, the one named last changes fastest.
Arguments:
- expert_hidden: bfloat16 [512, 8192], P(('grp', 'voc')), may hold values from -6 to 6
- expert_gain: float32 [8192], replicated, may hold values from 0.25 to 1.75
- expert_head: bfloat16 [128256, 8192], P('voc', 'grp'), may hold values from -0.2541165 to 0.2541165
- amateur_hidden: bfloat16 [512, 2048], P(('grp', 'voc')), may hold values from -6 to 6
- mlp_gain: float32 [2048], replicated, may hold values from 0.25 to 1.75
- gate_weight: bfloat16 [2048, 8192], P(None, 'voc'), may hold values from -0.125 to 0.125
- up_weight: bfloat16 [2048, 8192], P(None, 'voc'), may hold values from -0.125 to 0.125
- down_weight: bfloat16 [8192, 2048], P('voc'), may hold values from -0.25 to 0.25
- amateur_gain: float32 [2048], replicated, may hold values from 0.25 to 1.75
- amateur_embed: bfloat16 [128256, 2048], P('voc', 'grp'), may hold values from -0.508233 to 0.508233
- plausible: int32 [512, 256], P('grp'), may hold values from 0 to 128255
- targets: int32 [512], P('grp'), may hold values from 0 to 128255
Outputs:
- contrast: float32 [512, 256], P(('grp', 'voc'))
- entropy: float32 [512], P(('grp', 'voc'))
- target_score: float32 [512], P(('grp', 'voc'))
All inputs are finite; a program needn't handle non-finite values.
Results may differ from a plain program's by a relative error of at most 0.0063.
Values may be sent and summed in bfloat16 or wider, within the bound.
A program may use at most 192 MiB of HBM per device.

v0:
```python
import jax
import jax.numpy as jnp
from jax import lax
from jax.sharding import PartitionSpec as P

EPS = 1e-05
BETA = 0.5


def copy_for_each(x, axis):
    devices = lax.axis_size(axis)
    return lax.all_to_all(jnp.broadcast_to(x[None], (devices, *x.shape)), axis, 0, 0, tiled=True)


def laid_out(pieces, dim):
    dims = list(pieces.shape[1:])
    dims[dim] *= pieces.shape[0]
    return jnp.moveaxis(pieces, 0, dim).reshape(dims)


def collect(x, axis, dim):
    pieces = copy_for_each(x, axis)
    return laid_out(pieces, dim)


def in_blocks(x, dim, devices):
    before, after = (x.shape[:dim], x.shape[dim + 1 :])
    return jnp.moveaxis(x.reshape(*before, devices, -1, *after), dim, 0)


def sum_at_owner(x, axis, dim):
    pieces = in_blocks(x, dim, lax.axis_size(axis))
    arrived = lax.all_to_all(pieces, axis, split_axis=0, concat_axis=0, tiled=True)
    return arrived.sum(axis=0)


def in_one_piece(arrays, axis, dim, along):
    columns = [a.reshape(*a.shape[:along], -1) for a in arrays]
    both = jnp.concatenate(columns, axis=along)
    out, at, outs = (sum_at_owner(both, axis, dim), 0, [])
    for a, column in zip(arrays, columns):
        piece = out[..., at : at + column.shape[along]]
        outs.append(piece.reshape(*piece.shape[:along], *a.shape[along:]))
        at += column.shape[along]
    return tuple(outs)


def rms_scale(values, gain):
    return values * lax.rsqrt(jnp.mean(values * values, axis=-1, keepdims=True) + EPS) * gain


def times_rows(left, weight):
    return lax.dot_general(
        left, weight, (((1,), (1,)), ((), ())), preferred_element_type=jnp.float32
    )


def pick_flat(logits, local_ids):
    width = logits.shape[1]
    row_base = jnp.arange(logits.shape[0], dtype=jnp.int32)[:, None] * width
    flat_index = (row_base + local_ids).reshape(-1)
    return jnp.take(logits.reshape(-1), flat_index, axis=0).reshape(local_ids.shape)


def on_device(
    expert_hidden,
    expert_gain,
    expert_head,
    amateur_hidden,
    mlp_gain,
    gate_weight,
    up_weight,
    down_weight,
    amateur_gain,
    amateur_embed,
    plausible,
    targets,
):
    shard_rows = expert_head.shape[0]
    vocab_start = lax.axis_index("voc") * shard_rows
    normed = rms_scale(expert_hidden.astype(jnp.float32), expert_gain).astype(jnp.bfloat16)
    group_rows = lax.all_gather(normed, "voc", axis=0, tiled=True)
    columns = group_rows
    expert_logits = times_rows(columns, lax.all_gather(expert_head, "grp", axis=1, tiled=True))
    gathered = collect(amateur_hidden, "voc", 0)
    resid = gathered.astype(jnp.float32)
    mlp_in = rms_scale(resid, mlp_gain).astype(jnp.bfloat16)
    gate = jnp.dot(mlp_in, gate_weight, preferred_element_type=jnp.float32)
    upper = jnp.dot(mlp_in, up_weight, preferred_element_type=jnp.float32)
    inner = (jax.nn.silu(gate) * upper).astype(jnp.bfloat16)
    own_branch = sum_at_owner(
        jnp.dot(inner, down_weight, preferred_element_type=jnp.float32), "voc", 0
    )
    own_final = rms_scale(amateur_hidden.astype(jnp.float32) + own_branch, amateur_gain).astype(
        jnp.bfloat16
    )
    final_group = collect(own_final, "voc", 0)
    columns = final_group
    amateur_logits = times_rows(columns, lax.all_gather(amateur_embed, "grp", axis=1, tiled=True))
    exp_e = jnp.sum(jnp.exp(expert_logits), axis=1)
    exp_a = jnp.sum(jnp.exp(amateur_logits), axis=1)
    local_ids = plausible - vocab_start
    owned = (local_ids >= 0) & (local_ids < shard_rows)
    safe_ids = jnp.clip(local_ids, 0, shard_rows - 1)
    pick_e = jnp.where(owned, pick_flat(expert_logits, safe_ids), 0.0)
    pick_a = jnp.where(owned, pick_flat(amateur_logits, safe_ids), 0.0)
    local_target = targets[:, None] - vocab_start
    target_owned = (local_target >= 0) & (local_target < shard_rows)
    safe_target = jnp.clip(local_target, 0, shard_rows - 1)
    targ_e = jnp.where(target_owned, pick_flat(expert_logits, safe_target), 0.0)[:, 0]
    targ_a = jnp.where(target_owned, pick_flat(amateur_logits, safe_target), 0.0)[:, 0]
    total_e, total_a, own_pe, own_pa, own_te, own_ta = (
        sum_at_owner(exp_e, "voc", 0),
        *in_one_piece((exp_a, pick_e, pick_a, targ_e, targ_a), "voc", 0, 1),
    )
    lse_e = jnp.log(total_e)
    lse_a = jnp.log(total_a)
    scores = own_pe - lse_e[:, None] - BETA * (own_pa - lse_a[:, None])
    target_score = own_te - lse_e - BETA * (own_ta - lse_a)
    contrast = scores - jnp.log(jnp.sum(jnp.exp(scores), axis=1, keepdims=True))
    entropy = -jnp.sum(jnp.exp(contrast) * contrast, axis=1)
    return (contrast, entropy, target_score)


def solution(mesh):
    in_specs = (
        P(("grp", "voc"), None),
        P(),
        P("voc", "grp"),
        P(("grp", "voc"), None),
        P(),
        P(None, "voc"),
        P(None, "voc"),
        P("voc", None),
        P(),
        P("voc", "grp"),
        P("grp", None),
        P("grp"),
    )
    out_specs = (P(("grp", "voc"), None), P(("grp", "voc")), P(("grp", "voc")))
    return jax.shard_map(
        on_device, mesh=mesh, in_specs=in_specs, out_specs=out_specs, check_vma=False
    )
```

profile of v0, /device:TPU:0, one launch (start us, length us, event | category | flops | bytes accessed | tf_op | source)
XLA Modules:
  0.0 922.2 jit_solution(7792686293219438057)
XLA Ops:
  7.2 0.0 all-gather.5.cloned.1.call-start
  7.2 0.7 all-gather.5.cloned.1.call-update
  7.9 0.0 all-gather.9.cloned.1.call-start
  8.0 0.1 copy-done.5
  8.1 0.2 fusion.3
  8.3 0.7 fusion.11
  9.0 0.0 all-gather.9.cloned.1.call-update
  9.0 0.0 all-gather.7.cloned.1.call-start
  9.1 0.7 all-gather.7.cloned.1.call-update
  9.8 0.5 broadcast_in_dim.23
  10.3 30.2 %all_to_all.29 = bf16[64,4,2048]{2,1,0:T(4,128)(2,1)S(1)} all-to-all(bf16[64,4,2048]{2,1,0:T(4,128)(2,1)S(1)} %broadcast_in_dim.23), channel_id=1, replica_groups=mesh['grp'=2,'voc'=64] {'voc'}, dimensions={0} | all-to-all | bytes 2097152 | tf_op jit(solution)/shard_map/all_to_all | solution.py:12
  40.5 0.9 copy-done.2
  41.4 0.6 multiply_reduce_fusion
  42.1 0.1 rsqrt.28
  42.2 1.3 reshape.137
  43.5 0.5 fusion.20
  44.0 3.3 fusion.1
  47.2 2.9 reshape.129
  50.1 4.9 all-to-all-start.1
  55.0 0.1 add_bitcast_fusion
  55.1 0.1 copy.42
  55.3 28.7 %all-to-all-done.1 = f32[64,4,2048]{2,1,0:T(4,128)S(1)} async-done(((f32[64,4,2048]{2,1,0:T(4,128)}), f32[64,4,2048]{2,1,0:T(4,128)S(1)}, u32[]{:S(2)}, u32[]{:S(2)}) %all-to-all-start.1) | async-done | bytes 2097184 | tf_op jit(solution)/shard_map/all_to_all | solution.py:33
  84.0 0.4 reduce_sum.91
  84.3 0.1 multiply_reduce_fusion.1
  84.5 0.1 multiply_convert_fusion.1
  84.6 1.5 broadcast_in_dim.24
  86.0 5.8 all-to-all-start.2
  91.9 0.1 fusion.2
  91.9 19.2 %all-to-all-done.2 = bf16[64,4,2048]{2,1,0:T(4,128)(2,1)S(1)} async-done(((bf16[64,4,2048]{2,1,0:T(4,128)(2,1)}), bf16[64,4,2048]{2,1,0:T(4,128)(2,1)S(1)}, u32[]{:S(2)}, u32[]{:S(2)}) %all-to-all-start.2) | async-done | bytes 1048608 | tf_op jit(solution)/shard_map/all_to_all | solution.py:12
  111.1 1.1 reshape.130
  112.2 5.5 exponential_reduce_fusion.1
  117.7 1.9 copy.36
  119.6 3.4 reshape.134
  123.0 362.7 %gather_fusion.1 = f32[65536]{0:T(1024)S(1)} fusion(f32[513024]{0:T(1024)S(1)} %reshape.134, s32[65536]{0:T(1024)S(1)} %fusion.2), kind=kCustom, calls=%fused_computation.2.clone | custom fusion | bytes 786432 | tf_op jit(solution)/shard_map/jit(_take)/gather | solution.py:62
  485.7 0.1 broadcast_select_fusion
  485.8 0.1 reshape.135
  485.9 1.7 gather_fusion.3
  487.6 0.1 broadcast_select_fusion.2
  487.7 0.1 concatenate.16
  487.8 0.3 concatenate.20
  488.0 0.0 all-gather.9.cloned.1.call-done
  488.1 6.9 reshape.175
  494.9 15.8 %exponential_reduce_fusion = (f32[256]{0:T(256)S(1)}, f32[256,2004]{0,1:T(8,128)S(1)}) fusion(bf16[256,8192]{1,0:T(8,128)(2,1)} %reshape.175, bf16[2004,8192]{1,0:T(8,128)(2,1)} %all-gather.7.cloned.1.call-done), kind=kOutput, calls=%fused_computation.6 | convolution fusion | flops 8405898240 | bytes 39080960 | tf_op jit(solution)/shard_map/dot_general | solution.py:53
  510.7 1.9 copy.35
  512.6 3.4 reshape.131
  516.0 362.7 %gather_fusion = f32[65536]{0:T(1024)S(1)} fusion(f32[513024]{0:T(1024)S(1)} %reshape.131, s32[65536]{0:T(1024)S(1)} %fusion.2), kind=kCustom, calls=%fused_computation.clone | custom fusion | bytes 786432 | tf_op jit(solution)/shard_map/jit(_take)/gather | solution.py:62
  878.8 1.7 gather_fusion.2
  880.5 0.1 reshape.133
  880.6 0.7 all_to_all.22
  881.3 4.8 all-to-all-start.4
  886.2 0.1 concatenate.15
  886.2 0.3 concatenate.21
  886.5 0.3 concatenate.22
  886.8 1.6 concatenate.19
  888.4 7.3 all-to-all-done.4
  895.6 5.0 all-to-all-start.3
  900.6 0.1 reduce_sum.97
  900.7 12.6 %all-to-all-done.3 = f32[64,4,515]{2,1,0:T(4,128)S(1)} async-done(((f32[64,4,515]{2,1,0:T(4,128)}), f32[64,4,515]{2,1,0:T(4,128)S(1)}, u32[]{:S(2)}, u32[]{:S(2)}) %all-to-all-start.3) | async-done | bytes 527392 | tf_op jit(solution)/shard_map/all_to_all | solution.py:33
  913.2 0.1 reduce_sum.95
  913.4 0.2 slice_reduce_fusion
  913.6 0.5 subtract_subtract_fusion
  914.1 0.2 exponential_reduce_fusion.2
  914.3 0.8 fusion.13
  915.1 0.5 neg.8
  (34 shorter events, 0.2 us)
Async XLA Ops:
  7.2 36.8 %copy-start = (bf16[128,2048]{1,0:T(8,128)(2,1)S(1)}, bf16[128,2048]{1,0:T(8,128)(2,1)}, u32[]{:S(2)}) copy-start(bf16[128,2048]{1,0:T(8,128)(2,1)} %param.23) | copy-start | bytes 1572868
  7.2 0.9 copy-start.5
  7.2 1.1 copy-start.8
  7.2 105.0 %all-gather.5.cloned.1.call-start = ((), (), s32[]{:S(2)}) async-start(), calls=%async_computation.5 | async-start | bytes 12337152 | tf_op jit(solution)/shard_map/all_gather | solution.py:99
  7.9 480.1 %all-gather.9.cloned.1.call-start = ((), (), s32[]{:S(2)}) async-start(), calls=%async_computation.7 | async-start | bytes 4259840 | tf_op jit(solution)/shard_map/all_gather | solution.py:82
  9.0 0.8 copy-start.6
  9.0 485.9 %all-gather.7.cloned.1.call-start = ((), (), s32[]{:S(2)}) async-start(), calls=%async_computation.6 | async-start | bytes 49348608 | tf_op jit(solution)/shard_map/all_gather | solution.py:84
  40.5 1.0 copy-start.2
  41.4 2.0 copy-start.4
  41.4 2.1 copy-start.7
  50.1 4.9 copy-start.3
  50.1 5.2 copy-start.10
  50.1 33.9 %all-to-all-start.1 = ((f32[64,4,2048]{2,1,0:T(4,128)}), f32[64,4,2048]{2,1,0:T(4,128)S(1)}, u32[]{:S(2)}, u32[]{:S(2)}) async-start(f32[64,4,2048]{2,1,0:T(4,128)} %reshape.129), calls=%async_computation.1 | async-start | bytes 4194304 | tf_op jit(solution)/shard_map/all_to_all | solution.py:33
  55.0 29.5 %copy-start.9 = (f32[2048]{0:T(1024)S(1)}, f32[2048]{0:T(1024)}, u32[]{:S(2)}) copy-start(f32[2048]{0:T(1024)} %param.24) | copy-start | bytes 24580
  86.0 25.1 %all-to-all-start.2 = ((bf16[64,4,2048]{2,1,0:T(4,128)(2,1)}), bf16[64,4,2048]{2,1,0:T(4,128)(2,1)S(1)}, u32[]{:S(2)}, u32[]{:S(2)}) async-start(bf16[64,4,2048]{2,1,0:T(4,128)(2,1)} %broadcast_in_dim.24), calls=%async_computation.2 | async-start | bytes 2097152 | tf_op jit(solution)/shard_map/all_to_all | solution.py:12
  878.7 7.4 copy-start.11
  881.3 14.3 %all-to-all-start.4 = ((f32[64,1,4]{2,1,0:T(1,128)}), f32[64,1,4]{2,1,0:T(1,128)S(1)}, u32[]{:S(2)}, u32[]{:S(2)}) async-start(f32[64,1,4]{2,1,0:T(1,128)} %bitcast.1), calls=%async_computation.4 | async-start | bytes 65536 | tf_op jit(solution)/shard_map/all_to_all | solution.py:33
  886.1 29.5 %copy-start.1 = (bf16[128,2048]{1,0:T(8,128)(2,1)S(1)}, bf16[128,2048]{1,0:T(8,128)(2,1)}, u32[]{:S(2)}) copy-start(bf16[128,2048]{1,0:T(8,128)(2,1)} %param.23) | copy-start | bytes 1572868
  895.6 17.6 %all-to-all-start.3 = ((f32[64,4,515]{2,1,0:T(4,128)}), f32[64,4,515]{2,1,0:T(4,128)S(1)}, u32[]{:S(2)}, u32[]{:S(2)}) async-start(f32[64,4,515]{2,1,0:T(4,128)} %concatenate.19), calls=%async_computation.3 | async-start | bytes 1310720 | tf_op jit(solution)/shard_map/all_to_all | solution.py:33
Sparse Core Ops, SparseCore 0:
  9.7 24.7 all-gather.4
  37.4 95.2 all-gather.8
  134.3 50.4 all-gather.6
where the time goes:
time: 923 us; the launch traced here: 922 us
  local copies, waits for them, and re-layouts  758 us (82%)
  waiting for transfers between devices  69.1 us (7%)
  blocking collectives  30.2 us (3%)
  matrix products  25 us (3%)
  starting transfers between devices  20.5 us (2%)
  between operations  14.1 us (2%)
    gather x4, local copies, waits for them, and re-layouts, pick_flat(): jnp.take(logits.reshape(-1), flat_index, axis=0).reshape(local_ids.shape)  729 us
    all_to_all x3, waiting for transfers between devices, sum_at_owner(): lax.all_to_all(pieces, axis, split_axis=0, concat_axis=0, tiled=True)  48.5 us
    all_to_all x1, blocking collectives, copy_for_each(): lax.all_to_all(jnp.broadcast_to(x[None], (devices, *x.shape)), axis, 0, 0...  30.2 us
    dot_general x2, matrix products, times_rows(): lax.dot_general(left, weight, (((1,), (1,)), ((), ())), preferred_element...  21.3 us
    all_to_all x1, waiting for transfers between devices, copy_for_each(): lax.all_to_all(jnp.broadcast_to(x[None], (devices, *x.shape)), axis, 0, 0...  19.2 us
  transfers between devices with their start and end apart: 7, of which 4 were waited for; matrix products, arithmetic and copies ran while one was open for 43% of the time, Pallas kernels for 0%

commit v1 on v0

v1 whole, which is shorter than its diff:
```python
import functools

import jax
import jax.numpy as jnp
from jax import lax
from jax.experimental import pallas as pl
from jax.experimental.pallas import tpu as pltpu
from jax.sharding import PartitionSpec as P

EPS = 1e-05
BETA = 0.5
MESH = pl.DeviceIdType.MESH
TILE = 256
LANES = 128


def copy_for_each(x, axis):
    devices = lax.axis_size(axis)
    return lax.all_to_all(jnp.broadcast_to(x[None], (devices, *x.shape)), axis, 0, 0, tiled=True)


def in_blocks(x, dim, devices):
    before, after = (x.shape[:dim], x.shape[dim + 1 :])
    return jnp.moveaxis(x.reshape(*before, devices, -1, *after), dim, 0)


def sum_at_owner(x, axis, dim):
    pieces = in_blocks(x, dim, lax.axis_size(axis))
    arrived = lax.all_to_all(pieces, axis, split_axis=0, concat_axis=0, tiled=True)
    return arrived.sum(axis=0)


def rms_scale(values, gain):
    return values * lax.rsqrt(jnp.mean(values * values, axis=-1, keepdims=True) + EPS) * gain


def score_kernel(
    x_ref, a_ref, plaus_ref, targ_ref, head_hbm, embed_hbm, out_ref,
    head, embed, part_e, part_a, got_e, got_a, picked, sums,
    load_sem, send_sem, recv_sem,
):
    grp, voc = lax.axis_index("grp"), lax.axis_index("voc")
    peer = 1 - grp
    shard = head_hbm.shape[0]
    padded = head.shape[0]
    tiles = padded // TILE
    rows = plaus_ref.shape[0]
    whole = shard // 16 * 16

    head[whole:, :] = jnp.zeros((padded - whole, head.shape[1]), head.dtype)
    embed[whole:, :] = jnp.zeros((padded - whole, embed.shape[1]), embed.dtype)
    aligned = shard // 8 * 8
    loads = []
    for m, (src, dst) in enumerate(((head_hbm, head), (embed_hbm, embed))):
        spans = [(0, aligned)] + [(aligned, shard - aligned)] * (shard > aligned)
        loads.append([
            pltpu.make_async_copy(src.at[pl.ds(*s), :], dst.at[pl.ds(*s), :], load_sem.at[m, i])
            for i, s in enumerate(spans)
        ])
        for load in loads[m]:
            load.start()

    barrier = pltpu.get_barrier_semaphore()
    pl.semaphore_signal(barrier, inc=1, device_id={"grp": peer}, device_id_type=MESH)
    pl.semaphore_wait(barrier, 1)

    def exchange(m, j):
        part, got = ((part_e, got_e), (part_a, got_a))[m]
        return pltpu.make_async_remote_copy(
            src_ref=part.at[j, pl.ds(peer * rows, rows), :],
            dst_ref=got.at[j],
            send_sem=send_sem.at[m, j],
            recv_sem=recv_sem.at[m, j],
            device_id={"grp": peer},
            device_id_type=MESH,
        )

    def partial(m, left, weight, part):
        @pl.loop(0, tiles)
        def _(j):
            block = weight[pl.ds(pl.multiple_of(j * TILE, TILE), TILE), :]
            part[j] = lax.dot_general(
                left[...], block, (((1,), (1,)), ((), ())), preferred_element_type=jnp.float32
            )
            exchange(m, j).start()

    for load in loads[0]:
        load.wait()
    partial(0, x_ref, head, part_e)
    for load in loads[1]:
        load.wait()
    partial(1, a_ref, embed, part_a)

    picked[...] = jnp.zeros_like(picked)
    sums[...] = jnp.zeros_like(sums)
    target = targ_ref[...] - voc * shard
    lane = lax.broadcasted_iota(jnp.int32, (rows, LANES), 1)
    slots = plaus_ref.shape[1] // LANES
    own = pl.ds(grp * rows, rows)

    @pl.loop(0, tiles)
    def _(j):
        exchange(0, j).wait()
        exchange(1, j).wait()
        for half in range(TILE // LANES):
            at = pl.ds(half * LANES, LANES)
            expert = part_e[j, own, at] + got_e[j, :, at]
            amateur = part_a[j, own, at] + got_a[j, :, at]
            chunk = j * (TILE // LANES) + half
            column = chunk * LANES + lane
            valid = column < shard
            sums[0] += jnp.where(valid, jnp.exp(expert), 0.0)
            sums[1] += jnp.where(valid, jnp.exp(amateur), 0.0)
            both = jnp.where(valid, expert - BETA * amateur, 0.0)
            sums[2] += jnp.where(column == target, both, 0.0)
            for s in range(slots):
                local = plaus_ref[:, s * LANES : (s + 1) * LANES] - voc * shard
                found = jnp.take_along_axis(both, local & (LANES - 1), axis=1)
                here = (local >> 7 == chunk) & (local < shard)
                picked[s] = jnp.where(here, found, picked[s])

    for s in range(slots):
        out_ref[:, s * LANES : (s + 1) * LANES] = picked[s]
    total_e = jnp.sum(sums[0], axis=1, keepdims=True)
    total_a = jnp.sum(sums[1], axis=1, keepdims=True)
    at_target = jnp.sum(sums[2], axis=1, keepdims=True)
    tail = jnp.where(lane == 0, at_target, jnp.where(lane == 1, total_e, total_a))
    out_ref[:, slots * LANES :] = tail


def scores_of(x, a, plausible, targets, head, embed):
    rows, slots = plausible.shape
    padded = pl.cdiv(head.shape[0], TILE) * TILE
    tiles = padded // TILE
    vmem = pl.BlockSpec(memory_space=pltpu.VMEM)
    hbm = pl.BlockSpec(memory_space=pl.ANY)
    return pl.pallas_call(
        score_kernel,
        out_shape=jax.ShapeDtypeStruct((rows, slots + LANES), jnp.float32),
        in_specs=[vmem] * 4 + [hbm] * 2,
        out_specs=vmem,
        scratch_shapes=[
            pltpu.VMEM((padded, head.shape[1]), head.dtype),
            pltpu.VMEM((padded, embed.shape[1]), embed.dtype),
            pltpu.VMEM((tiles, 2 * rows, TILE), jnp.float32),
            pltpu.VMEM((tiles, 2 * rows, TILE), jnp.float32),
            pltpu.VMEM((tiles, rows, TILE), jnp.float32),
            pltpu.VMEM((tiles, rows, TILE), jnp.float32),
            pltpu.VMEM((slots // LANES, rows, LANES), jnp.float32),
            pltpu.VMEM((3, rows, LANES), jnp.float32),
            pltpu.SemaphoreType.DMA((2, 2)),
            pltpu.SemaphoreType.DMA((2, tiles)),
            pltpu.SemaphoreType.DMA((2, tiles)),
        ],
        compiler_params=pltpu.CompilerParams(
            collective_id=0, has_side_effects=True, vmem_limit_bytes=56 << 20
        ),
    )(x, a, plausible, targets, head, embed)


def half_width(rows):
    count, width = rows.shape
    halves = rows.reshape(count, 2, width // 2).swapaxes(0, 1)
    return lax.all_to_all(halves, "grp", 0, 0, tiled=True)


def all_rows(gathered):
    devices, groups, count, width = gathered.shape
    return gathered.swapaxes(0, 1).reshape(groups * devices * count, width)


def on_device(
    expert_hidden,
    expert_gain,
    expert_head,
    amateur_hidden,
    mlp_gain,
    gate_weight,
    up_weight,
    down_weight,
    amateur_gain,
    amateur_embed,
    plausible,
    targets,
):
    normed = rms_scale(expert_hidden.astype(jnp.float32), expert_gain).astype(jnp.bfloat16)
    expert_rows = all_rows(lax.all_gather(half_width(normed), "voc", axis=0))
    resid = copy_for_each(amateur_hidden, "voc").reshape(-1, amateur_hidden.shape[1])
    mlp_in = rms_scale(resid.astype(jnp.float32), mlp_gain).astype(jnp.bfloat16)
    gate = jnp.dot(mlp_in, gate_weight, preferred_element_type=jnp.float32)
    upper = jnp.dot(mlp_in, up_weight, preferred_element_type=jnp.float32)
    inner = (jax.nn.silu(gate) * upper).astype(jnp.bfloat16)
    own_branch = sum_at_owner(
        jnp.dot(inner, down_weight, preferred_element_type=jnp.float32), "voc", 0
    )
    own_final = rms_scale(amateur_hidden.astype(jnp.float32) + own_branch, amateur_gain).astype(
        jnp.bfloat16
    )
    amateur_rows = all_rows(copy_for_each(half_width(own_final), "voc"))
    found = scores_of(
        expert_rows, amateur_rows, plausible, targets[:, None], expert_head, amateur_embed
    )
    total = sum_at_owner(found, "voc", 0)
    slots = plausible.shape[1]
    lse_e = jnp.log(total[:, slots + 1])
    lse_a = jnp.log(total[:, slots + 2])
    shift = lse_e - BETA * lse_a
    scores = total[:, :slots] - shift[:, None]
    target_score = total[:, slots] - shift
    contrast = scores - jnp.log(jnp.sum(jnp.exp(scores), axis=1, keepdims=True))
    entropy = -jnp.sum(jnp.exp(contrast) * contrast, axis=1)
    return (contrast, entropy, target_score)


def solution(mesh):
    in_specs = (
        P(("grp", "voc"), None),
        P(),
        P("voc", "grp"),
        P(("grp", "voc"), None),
        P(),
        P(None, "voc"),
        P(None, "voc"),
        P("voc", None),
        P(),
        P("voc", "grp"),
        P("grp", None),
        P("grp"),
    )
    out_specs = (P(("grp", "voc"), None), P(("grp", "voc")), P(("grp", "voc")))
    return jax.shard_map(
        on_device, mesh=mesh, in_specs=in_specs, out_specs=out_specs, check_vma=False
    )
```

time: 923 us -> 195 us (0.21)
  local copies, waits for them, and re-layouts: 758 us -> 25.3 us
  blocking collectives: 30.2 us -> 90.4 us
  waiting for transfers between devices: 69.1 us -> 19.7 us
  Pallas kernels: 0 us -> 27.4 us
  matrix products: 25 us -> 3.71 us
  starting transfers between devices: 20.5 us -> 6.14 us
    gather x4 -> x0, local copies, waits for them, and re-layouts: 729 us -> none  [pick_flat(): jnp.take(logits.reshape(-1), flat_index, axis=0).reshape(local_ids.shape)]
    all_to_all x0 -> x4, blocking collectives: none -> 59.3 us  [the longest x2 51.1 us: sum_at_owner(): lax.all_to_all(pieces, axis, split_axis=0, concat_axis=0, tiled=True)]
    all_to_all x3 -> x0, waiting for transfers between devices: 48.5 us -> none  [sum_at_owner(): lax.all_to_all(pieces, axis, split_axis=0, concat_axis=0, tiled=True)]
    pallas_call x0 -> x1, Pallas kernels: none -> 27.4 us  [scores_of(): pl.pallas_call(score_kernel, out_shape=jax.ShapeDtypeStruct((rows, slots...]
    dot_general x2 -> x0, matrix products: 21.3 us -> none  [times_rows(): lax.dot_general(left, weight, (((1,), (1,)), ((), ())), preferred_element...]
    all_to_all x3 -> x0, starting transfers between devices: 14.6 us -> none  [sum_at_owner(): lax.all_to_all(pieces, axis, split_axis=0, concat_axis=0, tiled=True)]
  transfers between devices with their start and end apart: 7 -> 2, of which waited for: 4 -> 1; matrix products, arithmetic and copies ran while one was open for 43% -> 8% of each run, Pallas kernels for 0% -> 0%
where the time goes in v1:
time: 195 us; the launch traced here: 194 us
  blocking collectives  90.4 us (46%)
  Pallas kernels  27.4 us (14%)
  local copies, waits for them, and re-layouts  25.3 us (13%)
  waiting for transfers between devices  19.7 us (10%)
  between operations  14.2 us (7%)
  other arithmetic  7.11 us (4%)
  starting transfers between devices  6.14 us (3%)
  matrix products  3.71 us (2%)
    all_to_all x2, blocking collectives, sum_at_owner(): lax.all_to_all(pieces, axis, split_axis=0, concat_axis=0, tiled=True)  51.1 us
    all_to_all x1, blocking collectives, copy_for_each(): lax.all_to_all(jnp.broadcast_to(x[None], (devices, *x.shape)), axis, 0, 0...  31.1 us
    pallas_call x1, Pallas kernels, scores_of(): pl.pallas_call(score_kernel, out_shape=jax.ShapeDtypeStruct((rows, slots...  27.4 us
    all_to_all x1, waiting for transfers between devices, copy_for_each(): lax.all_to_all(jnp.broadcast_to(x[None], (devices, *x.shape)), axis, 0, 0...  19.7 us
    transpose x2, local copies, waits for them, and re-layouts, all_rows(): return gathered.swapaxes(0, 1).reshape(groups * devices * count, width)  8.24 us
    all_to_all x2, blocking collectives, half_width(): return lax.all_to_all(halves, 'grp', 0, 0, tiled=True)  8.19 us
    reshape x2, local copies, waits for them, and re-layouts, all_rows(): return gathered.swapaxes(0, 1).reshape(groups * devices * count, width)  8.13 us
    all_to_all x1, starting transfers between devices, copy_for_each(): lax.all_to_all(jnp.broadcast_to(x[None], (devices, *x.shape)), axis, 0, 0...  6.11 us
  transfers between devices with their start and end apart: 2, of which 1 were waited for; matrix products, arithmetic and copies ran while one was open for 8% of the time, Pallas kernels for 0%

profile of v1, /device:TPU:0, one launch (start us, length us, event | category | flops | bytes accessed | tf_op | source)
XLA Modules:
  0.0 194.0 jit_solution(15597976485394397747)
XLA Ops:
  7.2 0.0 copy-start
  7.2 0.0 all-gather.3.cloned.1.call-start
  7.2 1.1 fusion.2
  8.3 0.9 fusion.4
  9.3 4.5 %all_to_all.30 = bf16[2,4,4096]{2,1,0:T(4,128)(2,1)} all-to-all(bf16[2,4,4096]{2,1,0:T(4,128)(2,1)S(1)} %bitcast.16), channel_id=1, replica_groups=mesh['grp'=2,'voc'=64] {'grp'}, dimensions={0} | all-to-all | bytes 131072 | tf_op jit(solution)/shard_map/all_to_all | solution.py:164
  13.7 0.0 all-gather.3.cloned.1.call-update
  13.8 1.2 broadcast_in_dim.6
  15.0 31.1 %all_to_all.31 = bf16[64,4,2048]{2,1,0:T(4,128)(2,1)S(1)} all-to-all(bf16[64,4,2048]{2,1,0:T(4,128)(2,1)S(1)} %broadcast_in_dim.6), channel_id=1, replica_groups=mesh['grp'=2,'voc'=64] {'voc'}, dimensions={0} | all-to-all | bytes 2097152 | tf_op jit(solution)/shard_map/all_to_all | solution.py:19
  46.1 0.0 copy-start.1
  46.1 1.0 copy-done.1
  47.1 0.0 copy-start.2
  47.1 0.0 copy-start.4
  47.1 0.6 multiply_reduce_fusion
  47.7 0.1 rsqrt.29
  47.8 1.3 reshape.81
  49.1 0.0 copy-done.2
  49.1 0.0 copy-done.4
  49.1 0.5 fusion.18
  49.6 0.0 copy-done
  49.6 3.2 %fusion.1 = f32[256,2048]{1,0:T(8,128)} fusion(bf16[128,2048]{1,0:T(8,128)(2,1)S(1)} %copy-done, bf16[2048,128]{1,0:T(8,128)(2,1)} %param.18, f32[256,128]{1,0:T(8,128)S(1)} %fusion.18, f32[256,2048]{1,0:T(8,128)S(1)} %reshape.81, f32[2048]{0:T(1024)S(1)} %copy-done.4, f32[256]{0:T(256)S(1)} %rsqrt.29), kind=kOutput, calls=%fused_computation.4 | convolution fusion | flops 270204928 | bytes 5383168 | tf_op jit(solution)/shard_map/dot_general | solution.py:194
  52.9 1.9 %reshape.77 = f32[64,4,2048]{2,1,0:T(4,128)S(1)} reshape(f32[256,2048]{1,0:T(8,128)} %fusion.1) | data formatting | bytes 4194304 | tf_op jit(solution)/shard_map/reshape | solution.py:24
  54.8 34.6 %all_to_all.32 = f32[64,4,2048]{2,1,0:T(4,128)} all-to-all(f32[64,4,2048]{2,1,0:T(4,128)S(1)} %reshape.77), channel_id=1, replica_groups=mesh['grp'=2,'voc'=64] {'voc'}, dimensions={0} | all-to-all | bytes 4194304 | tf_op jit(solution)/shard_map/all_to_all | solution.py:29
  89.4 0.0 copy-start.3
  89.4 0.0 copy-start.5
  89.4 1.9 reduce_sum.65
  91.4 0.0 copy-done.3
  91.4 0.0 copy-start.6
  91.4 0.1 multiply_reduce_fusion.1
  91.5 0.0 copy-done.5
  91.6 0.1 multiply_convert_fusion.1
  91.6 3.7 %all_to_all.33 = bf16[2,4,1024]{2,1,0:T(4,128)(2,1)S(1)} all-to-all(bf16[2,4,1024]{2,1,0:T(4,128)(2,1)S(1)} %bitcast.17), channel_id=1, replica_groups=mesh['grp'=2,'voc'=64] {'grp'}, dimensions={0} | all-to-all | bytes 32768 | tf_op jit(solution)/shard_map/all_to_all | solution.py:164
  95.4 1.5 broadcast_in_dim.7
  96.8 6.1 %all-to-all-start.4 = ((bf16[64,2,4,1024]{3,2,1,0:T(4,128)(2,1)}), bf16[64,2,4,1024]{3,2,1,0:T(4,128)(2,1)S(1)}, u32[]{:S(2)}, u32[]{:S(2)}) async-start(bf16[64,2,4,1024]{3,2,1,0:T(4,128)(2,1)} %broadcast_in_dim.7), calls=%async_computation.4 | async-start | bytes 2097152 | tf_op jit(solution)/shard_map/all_to_all | solution.py:19
  103.0 0.0 copy-done.6
  103.0 0.8 copy.31.targ_ref
  103.8 19.7 %all-to-all-done.4 = bf16[64,2,4,1024]{3,2,1,0:T(4,128)(2,1)S(1)} async-done(((bf16[64,2,4,1024]{3,2,1,0:T(4,128)(2,1)}), bf16[64,2,4,1024]{3,2,1,0:T(4,128)(2,1)S(1)}, u32[]{:S(2)}, u32[]{:S(2)}) %all-to-all-start.4) | async-done | bytes 1048608 | tf_op jit(solution)/shard_map/all_to_all | solution.py:19
  123.5 0.4 copy.30
  123.8 1.2 reshape.79.a_ref
  125.1 0.0 all-gather.3.cloned.1.call-done
  125.1 7.9 %copy.27 = bf16[2,64,4,4096]{3,2,1,0:T(4,128)(2,1)} copy(bf16[2,64,4,4096]{3,2,0,1:T(4,128)(2,1)} %bitcast.14) | data formatting | bytes 8388608 | tf_op jit(solution)/shard_map/transpose | solution.py:169
  132.9 6.9 %reshape.76.x_ref = bf16[512,4096]{1,0:T(8,128)(2,1)} reshape(bf16[2,64,4,4096]{3,2,1,0:T(4,128)(2,1)} %copy.27) | data formatting | bytes 8388608 | tf_op jit(solution)/shard_map/reshape | solution.py:169
  139.9 27.4 %shard_map.139 = f32[256,384]{1,0:T(8,128)} custom-call(bf16[512,4096]{1,0:T(8,128)(2,1)} %reshape.76.x_ref, bf16[512,1024]{1,0:T(8,128)(2,1)} %reshape.79.a_ref, s32[256,256]{1,0:T(8,128)} %plaus_ref.1, s32[256,1]{1,0:T(8,128)} %copy.31.targ_ref, bf16[2004,4096]{1,0:T(8,128)(2,1)} %head_hbm.1, bf16[2004,1024]{1,0:T(8,128)(2,1)} %embed_hbm.1), custom_call_target="tpu_custom_call" | custom-call | tf_op jit(solution)/shard_map/pallas_call | solution.py:137
  167.2 1.1 reshape.80
  168.3 16.5 %all_to_all.34 = f32[64,4,384]{2,1,0:T(4,128)S(1)} all-to-all(f32[64,4,384]{2,1,0:T(4,128)S(1)} %reshape.80), channel_id=1, replica_groups=mesh['grp'=2,'voc'=64] {'voc'}, dimensions={0} | all-to-all | bytes 786432 | tf_op jit(solution)/shard_map/all_to_all | solution.py:29
  184.8 0.1 reduce_sum.67
  184.9 0.7 fusion.13
  185.6 0.2 exponential_reduce_fusion
  185.8 0.8 fusion.11
  186.6 0.5 neg.8
  (4 shorter events, 0.0 us)
Async XLA Ops:
  7.2 42.5 %copy-start = (bf16[128,2048]{1,0:T(8,128)(2,1)S(1)}, bf16[128,2048]{1,0:T(8,128)(2,1)}, u32[]{:S(2)}) copy-start(bf16[128,2048]{1,0:T(8,128)(2,1)} %param.19) | copy-start | bytes 1572868
  7.2 117.9 %all-gather.3.cloned.1.call-start = ((), (), s32[]{:S(2)}) async-start(), calls=%async_computation.6 | async-start | bytes 4259840 | tf_op jit(solution)/shard_map/all_gather | solution.py:187
  46.1 1.0 copy-start.1
  47.1 2.0 %copy-start.2 = (bf16[2048,128]{1,0:T(8,128)(2,1)S(1)}, bf16[2048,128]{1,0:T(8,128)(2,1)}, u32[]{:S(2)}) copy-start(bf16[2048,128]{1,0:T(8,128)(2,1)} %param.17) | copy-start | bytes 1572868
  47.1 2.1 %copy-start.4 = (f32[2048]{0:T(1024)S(1)}, f32[2048]{0:T(1024)}, u32[]{:S(2)}) copy-start(f32[2048]{0:T(1024)} %param.16) | copy-start | bytes 24580
  89.4 1.9 %copy-start.3 = (bf16[4,2048]{1,0:T(4,128)(2,1)S(1)}, bf16[4,2048]{1,0:T(4,128)(2,1)}, u32[]{:S(2)}) copy-start(bf16[4,2048]{1,0:T(4,128)(2,1)} %param.15) | copy-start | bytes 49156
  89.4 2.1 %copy-start.5 = (f32[2048]{0:T(1024)S(1)}, f32[2048]{0:T(1024)}, u32[]{:S(2)}) copy-start(f32[2048]{0:T(1024)} %param.20) | copy-start | bytes 24580
  91.4 11.6 %copy-start.6 = (s32[256]{0:T(256)S(1)}, s32[256]{0:T(256)}, u32[]{:S(2)}) copy-start(s32[256]{0:T(256)} %param.23) | copy-start | bytes 3076
  96.8 26.6 %all-to-all-start.4 = ((bf16[64,2,4,1024]{3,2,1,0:T(4,128)(2,1)}), bf16[64,2,4,1024]{3,2,1,0:T(4,128)(2,1)S(1)}, u32[]{:S(2)}, u32[]{:S(2)}) async-start(bf16[64,2,4,1024]{3,2,1,0:T(4,128)(2,1)} %broadcast_in_dim.7), calls=%async_computation.4 | async-start | bytes 2097152 | tf_op jit(solution)/shard_map/all_to_all | solution.py:19
Sparse Core Ops, SparseCore 0:
  13.9 103.2 all-gather.2

commit v2 on v1

v2 whole, which is shorter than its diff:
```python
import functools

import jax
import jax.numpy as jnp
from jax import lax
from jax.experimental import pallas as pl
from jax.experimental.pallas import tpu as pltpu
from jax.sharding import PartitionSpec as P

EPS = 1e-05
BETA = 0.5
MESH = pl.DeviceIdType.MESH
TILE = 256
LANES = 128
RING = 4
AXES = 3
OWN = 4


def rms_scale(values, gain):
    return values * lax.rsqrt(jnp.mean(values * values, axis=-1, keepdims=True) + EPS) * gain


def thirds(width):
    lanes, spans, at = width // LANES, [], 0
    for p in range(AXES):
        count = (lanes + p) // AXES * LANES
        spans.append((at, count))
        at += count
    return spans


def order_of(p):
    return [(p + s) % AXES for s in range(AXES)]


def slots_shape(p, s, columns):
    left = [axis for axis in range(AXES) if axis not in order_of(p)[: s + 1]]
    lead = [RING for axis in left if axis < 2]
    return (RING, *lead, OWN * RING if 2 in left else OWN, columns)


def reduce_buffers(width, dtype):
    spans = thirds(width)
    got = [[pltpu.VMEM(slots_shape(p, s, n), dtype) for p, (_, n) in enumerate(spans)] for s in range(3)]
    sums = [[pltpu.VMEM(slots_shape(p, s, n)[1:], dtype) for p, (_, n) in enumerate(spans)] for s in range(2)]
    sems = [pltpu.SemaphoreType.DMA((3, AXES, RING))] * 2
    return [got, sums, *sems]


class Torus:
    def __init__(self):
        self.grp, voc = lax.axis_index("grp"), lax.axis_index("voc")
        self.voc = voc
        self.me = (voc // (RING * RING), voc // RING % RING, voc % RING)
        self.sent = []

    def shifted(self, axis, d):
        place = [(c + d) % RING if a == axis else c for a, c in enumerate(self.me)]
        return (place[0] * RING + place[1]) * RING + place[2]

    def copy(self, src, dst, send, recv, grp, voc):
        made = pltpu.make_async_remote_copy(
            src_ref=src, dst_ref=dst, send_sem=send, recv_sem=recv,
            device_id={"grp": grp, "voc": voc}, device_id_type=MESH,
        )
        made.start()
        self.sent.append(made)
        return made

    def local(self, src, dst, sem):
        made = pltpu.make_async_copy(src, dst, sem)
        made.start()
        return made

    def greet(self):
        barrier = pltpu.get_barrier_semaphore()
        others = [(1 - self.grp, self.voc)]
        for axis in range(AXES):
            for d in range(1, RING):
                for grp in (self.grp, 1 - self.grp):
                    others.append((grp, self.shifted(axis, d)))
        for grp, voc in others:
            pl.semaphore_signal(
                barrier, inc=1, device_id={"grp": grp, "voc": voc}, device_id_type=MESH
            )
        pl.semaphore_wait(barrier, len(others))

    def gather_first(self, src, dst, sems, halves):
        send, recv = sems
        width = dst.shape[-1]
        z, y, x = self.me
        copies = []
        for p, (at, n) in enumerate(thirds(width)):
            lead = self.grp if halves else 0
            place = dst.at[lead, z, y, pl.ds(x * OWN, OWN), pl.ds(at, n)]
            for other in range(2 if halves else 1):
                grp = 1 - self.grp if other else self.grp
                start = pl.multiple_of(grp * width + at, LANES) if halves else at
                piece = src.at[:, pl.ds(start, n)]
                for d in range(RING):
                    k = other * RING + d
                    if k == 0:
                        copies.append(self.local(piece, place, recv.at[0, p, 0]))
                    else:
                        copies.append(
                            self.copy(
                                piece, place, send.at[0, p, k], recv.at[0, p, k],
                                grp, self.shifted(p, d),
                            )
                        )
        return copies

    def gather_next(self, s, dst, sems):
        send, recv = sems
        z, y, x = self.me
        copies = []
        for p, (at, n) in enumerate(thirds(dst.shape[-1])):
            order = order_of(p)
            done = order[:s]
            block = dst.at[
                :,
                pl.ds(0, RING) if 0 in done else pl.ds(z, 1),
                pl.ds(0, RING) if 1 in done else pl.ds(y, 1),
                pl.ds(0, RING * OWN) if 2 in done else pl.ds(x * OWN, OWN),
                pl.ds(at, n),
            ]
            for d in range(1, RING):
                copies.append(
                    self.copy(
                        block, block, send.at[s, p, d], recv.at[s, p, d],
                        self.grp, self.shifted(order[s], d),
                    )
                )
        return copies

    def reduce_stage(self, s, src, buffers, width):
        got, sums, send, recv = buffers
        copies = []
        for p, (at, n) in enumerate(thirds(width)):
            order = order_of(p)
            axis = order[s]
            left = [a for a in range(AXES) if a not in order[:s]]
            source = src if s == 0 else sums[s - 1][p]
            for d in range(RING):
                c = (self.me[axis] + d) % RING
                index = [c if a == axis else slice(None) for a in left if a < 2]
                index.append(pl.ds(c * OWN, OWN) if axis == 2 else slice(None))
                index.append(pl.ds(at, n) if s == 0 else slice(None))
                piece = source.at[tuple(index)]
                slot = got[s][p].at[self.me[axis]]
                if d == 0:
                    copies.append(self.local(piece, slot, recv.at[s, p, 0]))
                else:
                    copies.append(
                        self.copy(
                            piece, slot, send.at[s, p, d], recv.at[s, p, d],
                            self.grp, self.shifted(axis, d),
                        )
                    )
        return copies

    def reduce_scatter(self, src, buffers, result, meanwhile=None):
        got, sums, _, _ = buffers
        width = result.shape[-1]
        for s in range(3):
            copies = self.reduce_stage(s, src, buffers, width)
            if meanwhile is not None:
                meanwhile(s)
            arrived(copies)
            for p, (at, n) in enumerate(thirds(width)):
                total = got[s][p][0].astype(jnp.float32)
                for k in range(1, RING):
                    total += got[s][p][k].astype(jnp.float32)
                if s < 2:
                    sums[s][p][...] = total.astype(sums[s][p].dtype)
                else:
                    result[:, at : at + n] = total


def arrived(copies):
    for made in copies:
        if made.is_remote:
            made.wait_recv()
        else:
            made.wait()


def whole_kernel(
    hidden_ref, gain_ref, resid_ref, mlp_gain_ref, last_gain_ref, plaus_ref, targ_ref,
    gate_hbm, up_hbm, down_hbm, head_hbm, embed_hbm,
    out_ref, stat_ref,
    gate, up, down, head, embed, load_sem,
    normed, x_all, x_sems, h_all, h_sems, last, a_all, a_sems,
    branch, branch_buffers, summed,
    part_e, part_a, got_e, got_a, picked, sums, swap_send, swap_recv,
    found, found_buffers, total_ref,
):
    torus = Torus()
    grp, voc = torus.grp, torus.voc
    peer = 1 - grp
    shard = head_hbm.shape[0]
    padded = head.shape[0]
    tiles = padded // TILE
    rows = plaus_ref.shape[0]

    weights = [
        torus.local(src, dst, load_sem.at[i, 0])
        for i, (src, dst) in enumerate(((gate_hbm, gate), (up_hbm, up), (down_hbm, down)))
    ]
    torus.greet()

    copies_h = torus.gather_first(resid_ref, h_all, h_sems, False)
    normed[...] = rms_scale(hidden_ref[...].astype(jnp.float32), gain_ref[...]).astype(normed.dtype)
    copies_x = torus.gather_first(normed, x_all, x_sems, True)

    whole = shard // 16 * 16
    aligned = shard // 8 * 8
    loads = []
    for m, (src, dst) in enumerate(((head_hbm, head), (embed_hbm, embed))):
        dst[whole:, :] = jnp.zeros((padded - whole, dst.shape[1]), dst.dtype)
        spans = [(0, aligned)] + [(aligned, shard - aligned)] * (shard > aligned)
        loads.append([
            torus.local(src.at[pl.ds(*span), :], dst.at[pl.ds(*span), :], load_sem.at[3 + m, i])
            for i, span in enumerate(spans)
        ])

    arrived(copies_h)
    copies_h = torus.gather_next(1, h_all, h_sems)
    arrived(copies_x)
    copies_x = torus.gather_next(1, x_all, x_sems)
    arrived(copies_h)
    copies_h = torus.gather_next(2, h_all, h_sems)
    arrived(copies_x)
    copies_x = torus.gather_next(2, x_all, x_sems)
    arrived(weights)
    arrived(copies_h)

    hidden = h_all[...].reshape(rows, h_all.shape[-1]).astype(jnp.float32)
    mlp_in = rms_scale(hidden, mlp_gain_ref[...]).astype(jnp.bfloat16)
    gated = jnp.dot(mlp_in, gate[...], preferred_element_type=jnp.float32)
    upper = jnp.dot(mlp_in, up[...], preferred_element_type=jnp.float32)
    inner = (gated / (1.0 + jnp.exp(-gated)) * upper).astype(jnp.bfloat16)
    partial = jnp.dot(inner, down[...], preferred_element_type=jnp.float32)
    branch[...] = partial.astype(branch.dtype).reshape(branch.shape)
    torus.reduce_scatter(branch, branch_buffers, summed)

    final = resid_ref[...].astype(jnp.float32) + summed[...]
    last[...] = rms_scale(final, last_gain_ref[...]).astype(last.dtype)

    def exchange(m, j):
        part, got = ((part_e, got_e), (part_a, got_a))[m]
        return pltpu.make_async_remote_copy(
            src_ref=part.at[j, pl.ds(peer * rows, rows), :],
            dst_ref=got.at[j],
            send_sem=swap_send.at[m, j],
            recv_sem=swap_recv.at[m, j],
            device_id={"grp": peer, "voc": voc},
            device_id_type=MESH,
        )

    def partial_logits(m, first, stop):
        left, weight, part = ((x_all, head, part_e), (a_all, embed, part_a))[m]

        @pl.loop(first, stop)
        def _(j):
            block = weight[pl.ds(pl.multiple_of(j * TILE, TILE), TILE), :]
            part[j] = lax.dot_general(
                left[...].reshape(2 * rows, left.shape[-1]), block,
                (((1,), (1,)), ((), ())), preferred_element_type=jnp.float32,
            )
            exchange(m, j).start()

    copies_a = torus.gather_first(last, a_all, a_sems, True)
    arrived(copies_x)
    arrived(loads[0])
    cut = (0, tiles // 4, tiles // 2, tiles)
    for s in range(1, 3):
        partial_logits(0, cut[s - 1], cut[s])
        arrived(copies_a)
        copies_a = torus.gather_next(s, a_all, a_sems)
    partial_logits(0, cut[2], cut[3])
    arrived(copies_a)
    arrived(loads[1])
    partial_logits(1, 0, tiles)

    picked[...] = jnp.zeros_like(picked)
    sums[...] = jnp.zeros_like(sums)
    target = targ_ref[...] - voc * shard
    lane = lax.broadcasted_iota(jnp.int32, (rows, LANES), 1)
    slots = plaus_ref.shape[1] // LANES
    own = pl.ds(grp * rows, rows)

    @pl.loop(0, tiles)
    def _(j):
        exchange(0, j).wait()
        exchange(1, j).wait()
        for half in range(TILE // LANES):
            at = pl.ds(half * LANES, LANES)
            expert = part_e[j, own, at] + got_e[j, :, at]
            amateur = part_a[j, own, at] + got_a[j, :, at]
            chunk = j * (TILE // LANES) + half
            column = chunk * LANES + lane
            valid = column < shard
            sums[0] += jnp.where(valid, jnp.exp(expert), 0.0)
            sums[1] += jnp.where(valid, jnp.exp(amateur), 0.0)
            both = jnp.where(valid, expert - BETA * amateur, 0.0)
            sums[2] += jnp.where(column == target, both, 0.0)
            for s in range(slots):
                local = plaus_ref[:, s * LANES : (s + 1) * LANES] - voc * shard
                taken = jnp.take_along_axis(both, local & (LANES - 1), axis=1)
                here = (local >> 7 == chunk) & (local < shard)
                picked[s] = jnp.where(here, taken, picked[s])

    place = (*found.shape[:3], LANES)
    for s in range(slots):
        found[:, :, :, s * LANES : (s + 1) * LANES] = picked[s].reshape(place)
    total_e = jnp.sum(sums[0], axis=1, keepdims=True)
    total_a = jnp.sum(sums[1], axis=1, keepdims=True)
    at_target = jnp.sum(sums[2], axis=1, keepdims=True)
    tail = jnp.where(lane == 0, at_target, jnp.where(lane == 1, total_e, total_a))
    found[:, :, :, slots * LANES :] = tail.reshape(place)

    torus.reduce_scatter(found, found_buffers, total_ref)
    count = slots * LANES
    total = total_ref[...]
    shift = jnp.log(total[:, count + 1 : count + 2]) - BETA * jnp.log(total[:, count + 2 : count + 3])
    scores = total[:, :count] - shift
    contrast = scores - jnp.log(jnp.sum(jnp.exp(scores), axis=1, keepdims=True))
    out_ref[...] = contrast
    entropy = -jnp.sum(jnp.exp(contrast) * contrast, axis=1, keepdims=True)
    lane = lax.broadcasted_iota(jnp.int32, stat_ref.shape, 1)
    stat_ref[...] = jnp.where(lane == 0, entropy, total[:, count : count + 1] - shift)
    for made in torus.sent:
        made.wait_send()


def on_device(
    expert_hidden,
    expert_gain,
    expert_head,
    amateur_hidden,
    mlp_gain,
    gate_weight,
    up_weight,
    down_weight,
    amateur_gain,
    amateur_embed,
    plausible,
    targets,
):
    rows, slots = plausible.shape
    shard, wide = expert_head.shape
    narrow = amateur_embed.shape[1]
    width, units = gate_weight.shape
    padded = pl.cdiv(shard, TILE) * TILE
    tiles = padded // TILE
    bf16, f32 = jnp.bfloat16, jnp.float32
    vmem = pl.BlockSpec(memory_space=pltpu.VMEM)
    hbm = pl.BlockSpec(memory_space=pl.ANY)
    dma = pltpu.SemaphoreType.DMA
    stage_sems = [dma((3, AXES, 2 * RING))] * 2
    torus_rows = (RING, RING, RING * OWN)
    out, stats = pl.pallas_call(
        whole_kernel,
        out_shape=(
            jax.ShapeDtypeStruct((OWN, slots), f32),
            jax.ShapeDtypeStruct((OWN, LANES), f32),
        ),
        in_specs=[vmem] * 7 + [hbm] * 5,
        out_specs=(vmem, vmem),
        scratch_shapes=[
            pltpu.VMEM((width, units), bf16),
            pltpu.VMEM((width, units), bf16),
            pltpu.VMEM((units, width), bf16),
            pltpu.VMEM((padded, wide), bf16),
            pltpu.VMEM((padded, narrow), bf16),
            dma((5, 2)),
            pltpu.VMEM((OWN, 2 * wide), bf16),
            pltpu.VMEM((2, *torus_rows, wide), bf16),
            stage_sems,
            pltpu.VMEM((1, *torus_rows, width), bf16),
            stage_sems,
            pltpu.VMEM((OWN, width), bf16),
            pltpu.VMEM((2, *torus_rows, narrow), bf16),
            stage_sems,
            pltpu.VMEM((*torus_rows, width), bf16),
            reduce_buffers(width, bf16),
            pltpu.VMEM((OWN, width), f32),
            pltpu.VMEM((tiles, 2 * rows, TILE), f32),
            pltpu.VMEM((tiles, 2 * rows, TILE), f32),
            pltpu.VMEM((tiles, rows, TILE), f32),
            pltpu.VMEM((tiles, rows, TILE), f32),
            pltpu.VMEM((slots // LANES, rows, LANES), f32),
            pltpu.VMEM((3, rows, LANES), f32),
            dma((2, tiles)),
            dma((2, tiles)),
            pltpu.VMEM((*torus_rows, slots + LANES), f32),
            reduce_buffers(slots + LANES, f32),
            pltpu.VMEM((OWN, slots + LANES), f32),
        ],
        compiler_params=pltpu.CompilerParams(
            collective_id=0, has_side_effects=True, vmem_limit_bytes=60 << 20
        ),
    )(
        expert_hidden, expert_gain[None], amateur_hidden, mlp_gain[None], amateur_gain[None],
        plausible, targets[:, None], gate_weight, up_weight, down_weight, expert_head, amateur_embed,
    )
    return (out, stats[:, 0], stats[:, 1])


def solution(mesh):
    in_specs = (
        P(("grp", "voc"), None),
        P(),
        P("voc", "grp"),
        P(("grp", "voc"), None),
        P(),
        P(None, "voc"),
        P(None, "voc"),
        P("voc", None),
        P(),
        P("voc", "grp"),
        P("grp", None),
        P("grp"),
    )
    out_specs = (P(("grp", "voc"), None), P(("grp", "voc")), P(("grp", "voc")))
    return jax.shard_map(
        on_device, mesh=mesh, in_specs=in_specs, out_specs=out_specs, check_vma=False
    )
```

time: 195 us -> 93.9 us (0.48)
  blocking collectives: 90.4 us -> 0 us
  Pallas kernels: 27.4 us -> 88.8 us
  local copies, waits for them, and re-layouts: 25.3 us -> 4.21 us
  waiting for transfers between devices: 19.7 us -> 0 us
  between operations: 14.2 us -> 0.64 us
  other arithmetic: 7.11 us -> 0 us
  starting transfers between devices: 6.14 us -> 0 us
  matrix products: 3.71 us -> 0 us
    all_to_all x5 -> x0, blocking collectives: 90.4 us -> none  [the longest x2 51.1 us: sum_at_owner(): lax.all_to_all(pieces, axis, split_axis=0, concat_axis=0, tiled=True)]
    pallas_call x1, Pallas kernels: 27.4 us -> 88.8 us  [on_device(): pl.pallas_call(whole_kernel, out_shape=(jax.ShapeDtypeStruct((OWN, slots)...]
    all_to_all x1 -> x0, waiting for transfers between devices: 19.7 us -> none  [copy_for_each(): lax.all_to_all(jnp.broadcast_to(x[None], (devices, *x.shape)), axis, 0, 0...]
    reshape x4 -> x0, local copies, waits for them, and re-layouts: 11.2 us -> none  [the longest x2 8.13 us: all_rows(): return gathered.swapaxes(0, 1).reshape(groups * devices * count, width)]
    transpose x2 -> x0, local copies, waits for them, and re-layouts: 8.24 us -> none  [all_rows(): return gathered.swapaxes(0, 1).reshape(groups * devices * count, width)]
    all_to_all x1 -> x0, starting transfers between devices: 6.11 us -> none  [copy_for_each(): lax.all_to_all(jnp.broadcast_to(x[None], (devices, *x.shape)), axis, 0, 0...]
    reduce_sum x7 -> x0, other arithmetic: 4.82 us -> none  [the longest x2 2.03 us: sum_at_owner(): return arrived.sum(axis=0)]
    dot_general x2 -> x0, matrix products: 3.71 us -> none  [the longest x1 3.21 us: on_device(): jnp.dot(inner, down_weight, preferred_element_type=jnp.float32)]
  transfers between devices with their start and end apart: 2 -> 0, of which waited for: 1 -> 0; matrix products, arithmetic and copies ran while one was open for 8% -> 0% of each run, Pallas kernels for 0% -> 0%
where the time goes in v2:
time: 93.9 us; the launch traced here: 93.7 us
  Pallas kernels  88.8 us (95%)
  local copies, waits for them, and re-layouts  4.21 us (4%)
    pallas_call x1, Pallas kernels, on_device(): pl.pallas_call(whole_kernel, out_shape=(jax.ShapeDtypeStruct((OWN, slots)...  88.8 us

profile of v2, /device:TPU:0, one launch (start us, length us, event | category | flops | bytes accessed | tf_op | source)
XLA Modules:
  0.0 93.7 jit_solution(12105807687109054135)
XLA Ops:
  0.6 1.5 %copy.15.targ_ref = s32[256,1]{1,0:T(8,128)} copy(s32[256,1]{0,1:T(1,128)} %bitcast.7) | data formatting | bytes 2048 | tf_op jit(solution)/shard_map/broadcast_in_dim | solution.py:407
  2.1 88.8 %shard_map.139 = (f32[4,256]{1,0:T(4,128)}, f32[4,128]{1,0:T(4,128)}) custom-call(bf16[4,8192]{1,0:T(4,128)(2,1)} %hidden_ref.1, f32[1,8192]{1,0:T(1,128)} %bitcast.4, bf16[4,2048]{1,0:T(4,128)(2,1)} %resid_ref.1, f32[1,2048]{1,0:T(1,128)} %bitcast.5, f32[1,2048]{1,0:T(1,128)} %bitcast.6, s32[256,256]{1,0:T(8,128)} %plaus_ref.1, s32[256,1]{1,0:T(8,128)} %copy.15.targ_ref, ...), custom_call_target="tpu_custom_call" | custom-call | tf_op jit(solution)/shard_map/pallas_call | solution.py:364
  90.9 1.5 %slice_reduce_fusion = (f32[4]{0:T(128)}, f32[4]{0:T(128)}) fusion(f32[4,128]{1,0:T(4,128)} %get-tuple-element.6), kind=kLoop, calls=%fused_computation | loop fusion | bytes 64 | tf_op jit(solution)/shard_map/slice | solution.py:409
  92.4 1.3 %copy.17 = f32[4,256]{1,0:T(4,128)} copy(f32[4,256]{1,0:T(4,128)} %get-tuple-element.12) | data formatting | bytes 8192

commit v3 on v2

--- a/solution.py
+++ b/solution.py
@@ -10,7 +10,7 @@
 EPS = 1e-05
 BETA = 0.5
 MESH = pl.DeviceIdType.MESH
-TILE = 256
+TILE = 512
 LANES = 128
 RING = 4
 AXES = 3
@@ -85,6 +85,12 @@
                 barrier, inc=1, device_id={"grp": grp, "voc": voc}, device_id_type=MESH
             )
         pl.semaphore_wait(barrier, len(others))
+
+    def drain(self, keep=0):
+        count = len(self.sent) - keep
+        for made in self.sent[:count]:
+            made.wait_send()
+        del self.sent[:count]
 
     def gather_first(self, src, dst, sems, halves):
         send, recv = sems
@@ -131,6 +137,28 @@
                         block, block, send.at[s, p, d], recv.at[s, p, d],
                         self.grp, self.shifted(order[s], d),
                     )
+                )
+        return copies
+
+    def gather_last(self, dst, sems, step, before=None):
+        send, recv = sems
+        copies = []
+        for p, (at, n) in enumerate(thirds(dst.shape[-1])):
+            axis = order_of(p)[2]
+
+            def block(lead, c):
+                index = [pl.ds(0, RING), pl.ds(0, RING), pl.ds(0, RING * OWN)]
+                index[axis] = pl.ds(c * OWN, OWN) if axis == 2 else pl.ds(c, 1)
+                return dst.at[(lead, *index, pl.ds(at, n))]
+
+            for way, d in enumerate((1, RING - 1)):
+                if step == 0:
+                    k, piece = d, block(slice(None), self.me[axis])
+                else:
+                    before[2 * p + way].wait_recv()
+                    k, piece = RING + way, block(pl.ds(way, 1), (self.me[axis] + RING - d) % RING)
+                copies.append(
+                    self.copy(piece, piece, send.at[2, p, k], recv.at[2, p, k], self.grp, self.shifted(axis, d))
                 )
         return copies
 
@@ -227,14 +255,14 @@
 
     arrived(copies_h)
     copies_h = torus.gather_next(1, h_all, h_sems)
-    arrived(copies_x)
-    copies_x = torus.gather_next(1, x_all, x_sems)
     arrived(copies_h)
     copies_h = torus.gather_next(2, h_all, h_sems)
     arrived(copies_x)
-    copies_x = torus.gather_next(2, x_all, x_sems)
+    copies_x = torus.gather_next(1, x_all, x_sems)
     arrived(weights)
     arrived(copies_h)
+    arrived(copies_x)
+    straight = torus.gather_last(x_all, x_sems, 0)
 
     hidden = h_all[...].reshape(rows, h_all.shape[-1]).astype(jnp.float32)
     mlp_in = rms_scale(hidden, mlp_gain_ref[...]).astype(jnp.bfloat16)
@@ -243,7 +271,13 @@
     inner = (gated / (1.0 + jnp.exp(-gated)) * upper).astype(jnp.bfloat16)
     partial = jnp.dot(inner, down[...], preferred_element_type=jnp.float32)
     branch[...] = partial.astype(branch.dtype).reshape(branch.shape)
-    torus.reduce_scatter(branch, branch_buffers, summed)
+    relayed = []
+
+    def pass_on(s):
+        if s == 1:
+            relayed.extend(torus.gather_last(x_all, x_sems, 1, straight))
+
+    torus.reduce_scatter(branch, branch_buffers, summed, pass_on)
 
     final = resid_ref[...].astype(jnp.float32) + summed[...]
     last[...] = rms_scale(final, last_gain_ref[...]).astype(last.dtype)
@@ -272,7 +306,7 @@
             exchange(m, j).start()
 
     copies_a = torus.gather_first(last, a_all, a_sems, True)
-    arrived(copies_x)
+    arrived(relayed)
     arrived(loads[0])
     cut = (0, tiles // 4, tiles // 2, tiles)
     for s in range(1, 3):
@@ -286,7 +320,7 @@
 
     picked[...] = jnp.zeros_like(picked)
     sums[...] = jnp.zeros_like(sums)
-    target = targ_ref[...] - voc * shard
+    target = jnp.broadcast_to(targ_ref[...], (LANES, rows)).T - voc * shard
     lane = lax.broadcasted_iota(jnp.int32, (rows, LANES), 1)
     slots = plaus_ref.shape[1] // LANES
     own = pl.ds(grp * rows, rows)
@@ -321,7 +355,7 @@
     tail = jnp.where(lane == 0, at_target, jnp.where(lane == 1, total_e, total_a))
     found[:, :, :, slots * LANES :] = tail.reshape(place)
 
-    torus.reduce_scatter(found, found_buffers, total_ref)
+    torus.reduce_scatter(found, found_buffers, total_ref, lambda s: torus.drain(AXES * (RING - 1)))
     count = slots * LANES
     total = total_ref[...]
     shift = jnp.log(total[:, count + 1 : count + 2]) - BETA * jnp.log(total[:, count + 2 : count + 3])
@@ -331,8 +365,7 @@
     entropy = -jnp.sum(jnp.exp(contrast) * contrast, axis=1, keepdims=True)
     lane = lax.broadcasted_iota(jnp.int32, stat_ref.shape, 1)
     stat_ref[...] = jnp.where(lane == 0, entropy, total[:, count : count + 1] - shift)
-    for made in torus.sent:
-        made.wait_send()
+    torus.drain()
 
 
 def on_device(
@@ -404,7 +437,7 @@
         ),
     )(
         expert_hidden, expert_gain[None], amateur_hidden, mlp_gain[None], amateur_gain[None],
-        plausible, targets[:, None], gate_weight, up_weight, down_weight, expert_head, amateur_embed,
+        plausible, targets[None], gate_weight, up_weight, down_weight, expert_head, amateur_embed,
     )
     return (out, stats[:, 0], stats[:, 1])
 

time: 93.9 us -> 85.3 us (0.908)
  Pallas kernels: 88.8 us -> 81.7 us
  local copies, waits for them, and re-layouts: 4.21 us -> 2.75 us
    pallas_call x1, Pallas kernels: 88.8 us -> 81.7 us  [on_device(): pl.pallas_call(whole_kernel, out_shape=(jax.ShapeDtypeStruct((OWN, slots)...]
    broadcast_in_dim x1 -> x0, local copies, waits for them, and re-layouts: 1.46 us -> none  [on_device(): targets[:, None]]
where the time goes in v3:
time: 85.3 us; the launch traced here: 85.1 us
  Pallas kernels  81.7 us (96%)
  local copies, waits for them, and re-layouts  2.75 us (3%)
    pallas_call x1, Pallas kernels, on_device(): pl.pallas_call(whole_kernel, out_shape=(jax.ShapeDtypeStruct((OWN, slots)...  81.7 us

profile of v3, /device:TPU:0, one launch (start us, length us, event | category | flops | bytes accessed | tf_op | source)
XLA Modules:
  0.0 85.1 jit_solution(2239830946654482141)
XLA Ops:
  0.6 81.7 %shard_map.139 = (f32[4,256]{1,0:T(4,128)}, f32[4,128]{1,0:T(4,128)}) custom-call(bf16[4,8192]{1,0:T(4,128)(2,1)} %hidden_ref.1, f32[1,8192]{1,0:T(1,128)} %bitcast.4, bf16[4,2048]{1,0:T(4,128)(2,1)} %resid_ref.1, f32[1,2048]{1,0:T(1,128)} %bitcast.5, f32[1,2048]{1,0:T(1,128)} %bitcast.6, s32[256,256]{1,0:T(8,128)} %plaus_ref.1, s32[1,256]{1,0:T(1,128)} %bitcast.7, ...), custom_call_target="tpu_custom_call" | custom-call | tf_op jit(solution)/shard_map/pallas_call | solution.py:397
  82.4 1.5 %slice_reduce_fusion = (f32[4]{0:T(128)}, f32[4]{0:T(128)}) fusion(f32[4,128]{1,0:T(4,128)} %get-tuple-element.6), kind=kLoop, calls=%fused_computation | loop fusion | bytes 64 | tf_op jit(solution)/shard_map/slice | solution.py:442
  83.9 1.3 %copy.16 = f32[4,256]{1,0:T(4,128)} copy(f32[4,256]{1,0:T(4,128)} %get-tuple-element.12) | data formatting | bytes 8192
